TPU v7x, 512 devices: a whole 4x8x8 slice. The times are simulated.
512 devices in a mesh: row: 32 (over z_hi, y, core), col: 16 (over x, z_lo).
Axes of the slice: x: 4, y: 8, z: 8 (z_hi: 2, z_lo: 4; z = z_hi * 4 + z_lo), core: 2. Of those that a mesh axis runs over, the one named last changes fastest.
Arguments:
- object_re: float32 [12288, 8192], P('row', 'col'), may hold values from -6 to 6
- object_im: float32 [12288, 8192], P('row', 'col'), may hold values from -6 to 6
- probe_re: float32 [256, 256], replicated, may hold values from -6 to 6
- probe_im: float32 [256, 256], replicated, may hold values from -6 to 6
- frames: bfloat16 [32, 16, 8, 256, 256], P('row', 'col'), may hold values from 0.049804688 to 20
- counts: int32 [32, 16], P('row', 'col'), may hold values from 1 to 8, as said below
- offsets: int32 [32, 16, 8, 2], P('row', 'col'), may hold values from -32 to 288, as said below
- frame_index: int32 [32, 16, 8], P('row', 'col'), may hold values from 0 to 7
Outputs:
- new_re: float32 [12288, 8192], P('row', 'col')
- new_im: float32 [12288, 8192], P('row', 'col')
Inputs may be any that keep to these rules, and one draw needn't show every extreme that they name: `counts`: in every draw some tile has 8 positions and some tile has one. Row offsets are -32 plus multiples of 16, at most 160; column offsets likewise, at most 288; in every draw some live position has both offsets at the lowest value and some has both at the highest.
All inputs are finite; a program needn't handle non-finite values.
Results may differ from a plain program's by a relative error of at most 0.0003.
Values sent between devices are 32-bit elements; how exact they have to be, the bound alone decides.
A program may use at most 64 MiB of HBM per device.

v0:
```python
import jax
import jax.numpy as jnp
import numpy as np
from jax import lax
from jax.experimental import pallas as pl
from jax.experimental.pallas import tpu as pltpu
from jax.sharding import PartitionSpec as P

F32, BF16 = jnp.float32, jnp.bfloat16
HALO, TR, TC, PS, SLOTS = 32, 384, 512, 256, 8
WIDE = TR + 2 * HALO
SIDES = ((-1, 0), (1, 0), (0, -1), (0, 1), (-1, -1), (-1, 1), (1, -1), (1, 1))
BACK = tuple(SIDES.index((-r, -c)) for r, c in SIDES)


def tables():
    n = np.arange(128)[:, None]
    k = np.arange(128)[None, :]
    out = []
    for angle in (2 * np.pi * (n * k % 128) / 128, 2 * np.pi * (n * (2 * k + 1) % 256) / 256):
        c, s = np.cos(angle) / 16, np.sin(angle) / 16
        m = np.block([[c, -s], [s, c]])
        out += [m, m.T]
    full = np.stack(out)
    hi = full.astype(np.float32).astype(BF16)
    lo = (full - hi.astype(np.float64)).astype(np.float32).astype(BF16)
    return np.stack([hi, lo], axis=1)


def split(x):
    hi = x.astype(BF16)
    lo = (x - hi.astype(F32)).astype(BF16)
    return hi, lo


def dot(a, b):
    return jnp.dot(a, b, preferred_element_type=F32)


def right(x, tab, t):
    hi, lo = split(x)
    th, tl = tab[t, 0], tab[t, 1]
    return dot(jnp.concatenate([hi, lo, hi], 1), jnp.concatenate([th, th, tl], 0))


def left(x, tab, t):
    hi, lo = split(x)
    th, tl = tab[t, 0], tab[t, 1]
    return dot(jnp.concatenate([th, th, tl], 1), jnp.concatenate([hi, lo, hi], 0))


def slot_terms(blocks, wr, wi, amp, tab):
    e_re = [wr[b] * blocks[0][b] - wi[b] * blocks[1][b] for b in (0, 1)]
    e_im = [wr[b] * blocks[1][b] + wi[b] * blocks[0][b] for b in (0, 1)]
    even = right(jnp.concatenate([e_re[0] + e_re[1], e_im[0] + e_im[1]], 1), tab, 0)
    odd = right(jnp.concatenate([e_re[0] - e_re[1], e_im[0] - e_im[1]], 1), tab, 2)

    def halves(op):
        a, b = op(even[:128], even[128:]), op(odd[:128], odd[128:])
        re = jnp.concatenate([a[:, :128], b[:, :128]], 1)
        im = jnp.concatenate([a[:, 128:], b[:, 128:]], 1)
        return jnp.concatenate([re, im], 0)

    u = left(halves(lambda p, q: p + q), tab, 1)
    v = left(halves(lambda p, q: p - q), tab, 3)

    def scaled(f, a):
        re, im = f[:128], f[128:]
        factor = 1.0 - a * lax.rsqrt(jnp.maximum(re * re + im * im, 0.25))
        return jnp.concatenate([re * factor, im * factor], 0)

    a = left(scaled(u, amp[:128]), tab, 0)
    b = left(scaled(v, amp[128:]), tab, 2)
    top, bot = a + b, a - b
    re = jnp.concatenate([top[:128], bot[:128]], 0)
    im = jnp.concatenate([top[128:], bot[128:]], 0)
    a = right(jnp.concatenate([re[:, :128], im[:, :128]], 1), tab, 1)
    b = right(jnp.concatenate([re[:, 128:], im[:, 128:]], 1), tab, 3)
    back = (a + b, a - b)
    t_re = [wr[i] * back[i][:, :128] + wi[i] * back[i][:, 128:] for i in (0, 1)]
    t_im = [wr[i] * back[i][:, 128:] - wi[i] * back[i][:, :128] for i in (0, 1)]
    return t_re, t_im


def permuted_amp(frame):
    r = lax.broadcasted_iota(jnp.int32, (PS, PS), 0)
    c = lax.broadcasted_iota(jnp.int32, (PS, PS), 1)

    def order(j):
        return jnp.where(j < 128, 2 * j, 2 * j - 255)

    cols = (r == order(c)).astype(F32).astype(BF16)
    rows = (c == order(r)).astype(F32).astype(BF16)
    return jnp.sqrt(dot(rows, dot(frame, cols).astype(BF16)))


def lanes(rows):
    return lax.broadcasted_iota(jnp.int32, (rows, 128), 1)


def turned(x, by):
    return pltpu.roll(x, by % 128, 1) if by % 128 else x


def pack(x, high):
    rows = x.shape[0] // 4
    lane = lanes(rows)
    out = None
    for g in range(4):
        piece = turned(x[rows * g : rows * (g + 1)], 32 * (g + 1) if high else 32 * g)
        out = piece if out is None else jnp.where(lane >= 32 * g, piece, out)
    return out


def unpack(x, high):
    return jnp.concatenate([turned(x, 96 - 32 * g if high else -32 * g) for g in range(4)], 0)


def kernel(
    count_ref, off_ref, idx_ref, obj_re, obj_im, probe_re, probe_im, frames_hbm, tab_hbm,
    new_re, new_im,
    po, acc, light, term, amp, wave, turns, frames, tab, probe,
    side_out, side_in, corner_out, corner_in,
    lrow_in, lside_out, lside_in, lcorner_out, lcorner_in,
    grow_in, gside_out, gside_in, gcorner_out, gcorner_in,
    local_sem, send_sem, recv_sem,
):
    row, col = lax.axis_index("row"), lax.axis_index("col")
    n_row, n_col = lax.axis_size("row"), lax.axis_size("col")
    peers = [(row + dr, col + dc) for dr, dc in SIDES]
    there = []
    for dr, dc in SIDES:
        ok = []
        if dr:
            ok.append(row > 0 if dr < 0 else row < n_row - 1)
        if dc:
            ok.append(col > 0 if dc < 0 else col < n_col - 1)
        there.append(ok[0] if len(ok) == 1 else ok[0] & ok[1])

    barrier = pltpu.get_barrier_semaphore()
    for k in range(8):
        @pl.when(there[k])
        def _():
            pl.semaphore_signal(barrier, inc=1, device_id=peers[k], device_id_type=pl.DeviceIdType.MESH)

    loads = []
    for b in range(4):
        for i, source in enumerate((obj_re, obj_im)):
            loads.append((source.at[:, :, pl.ds(128 * b, 128)], po.at[i, b, 2:26]))
    loads += [(probe_re, probe.at[0]), (probe_im, probe.at[1]), (frames_hbm, frames), (tab_hbm, tab)]
    loads = [pltpu.make_async_copy(s, d, local_sem.at[i]) for i, (s, d) in enumerate(loads)]
    for load in loads:
        load.start()

    for k, (dr, dc) in enumerate(SIDES):
        @pl.when(jnp.logical_not(there[k]))
        def _():
            if dc == 0:
                at = 0 if dr < 0 else HALO + TR
                po[:, 0:4, at // 16 : at // 16 + 2] = jnp.zeros((2, 4, 2, 16, 128), F32)
                h = 0 if dr < 0 else 1
                lrow_in[h] = jnp.zeros((1, 4, HALO, 128), F32)
                grow_in[h] = jnp.zeros((2, 4, HALO, 128), F32)
            elif dr == 0:
                for ref in (side_in, lside_in, gside_in):
                    ref[k - 2] = jnp.zeros(ref.shape[1:], F32)
            else:
                for ref in (corner_in, lcorner_in, gcorner_in):
                    ref[k - 4] = jnp.zeros(ref.shape[1:], F32)

    acc[...] = jnp.zeros_like(acc)
    light[...] = jnp.zeros_like(light)
    term[:, :, 0:12] = jnp.zeros((2, 2, 12, 16, 128), F32)
    term[:, :, 28:40] = jnp.zeros((2, 2, 12, 16, 128), F32)

    def message(phase, k, source, target):
        return pltpu.make_async_remote_copy(
            src_ref=source,
            dst_ref=target,
            send_sem=send_sem.at[phase, k],
            recv_sem=recv_sem.at[phase, BACK[k]],
            device_id=peers[k],
            device_id_type=pl.DeviceIdType.MESH,
        )

    def messages(phase, rows_of, side_o, side_i, corner_o, corner_i):
        out = []
        for k, (dr, dc) in enumerate(SIDES):
            j = BACK[k]
            if dc == 0:
                out.append(message(phase, k, *rows_of(k)))
            elif dr == 0:
                out.append(message(phase, k, side_o.at[k - 2], side_i.at[j - 2]))
            else:
                out.append(message(phase, k, corner_o.at[k - 4], corner_i.at[j - 4]))
        return out

    def start(group):
        for k in range(8):
            @pl.when(there[k])
            def _():
                group[k].start()

    def arrive(group):
        for k in range(8):
            @pl.when(there[k])
            def _():
                group[BACK[k]].wait_recv()

    def drain(group):
        for k in range(8):
            @pl.when(there[k])
            def _():
                group[k].wait_send()

    def object_rows(k):
        if k == 0:
            return po.at[:, 0:4, 2:4], po.at[:, 0:4, 26:28]
        return po.at[:, 0:4, 24:26], po.at[:, 0:4, 0:2]

    def spilled_rows(ref, into):
        def rows_of(k):
            at = 0 if k == 0 else HALO + TR
            return ref.at[:, 0:4, at : at + HALO, :], into.at[1 - k]
        return rows_of

    objects = messages(0, object_rows, side_out, side_in, corner_out, corner_in)
    lights = messages(1, spilled_rows(light, lrow_in), lside_out, lside_in, lcorner_out, lcorner_in)
    grads = messages(2, spilled_rows(acc, grow_in), gside_out, gside_in, gcorner_out, gcorner_in)

    for load in loads[:8]:
        load.wait()
    for i in range(2):
        side_out[0, i] = pack(po[i, 0, 2:26].reshape(TR, 128), False)
        side_out[1, i] = pack(po[i, 3, 2:26].reshape(TR, 128), True)
        for k in range(4, 8):
            dr, dc = SIDES[k]
            at = 2 if dr < 0 else 24
            corner_out[k - 4, i] = pack(po[i, 0 if dc < 0 else 3, at : at + 2].reshape(HALO, 128), dc > 0)

    neighbours = sum(t.astype(jnp.int32) for t in there)
    pl.semaphore_wait(barrier, neighbours)
    start(objects)
    for load in loads[8:]:
        load.wait()

    for i in range(2):
        for h in range(2):
            for k in range(8):
                turns[k, i, h] = turned(probe[i, :, 128 * h : 128 * h + 128], 16 * k)
    count = count_ref[0, 0]

    def place(s):
        p = lax.div(off_ref[0, s] + HALO, 16)
        c = off_ref[1, s]
        live = lax.max(lax.min(count - s, 1), 0)
        return p, c, c + PS * live

    def add(into, i, p, c, end):
        rows = pl.ds(12 - p, 28)
        lane = lanes(WIDE)
        cols = [lane + 128 * b for b in range(4)] + [jnp.where(lane < 64, lane + 512, lane - 128)]
        got = [term[i, h, rows].reshape(WIDE, 128) for h in range(2)]
        for b, at in enumerate(cols):
            source = got[b % 2] if b < 4 else jnp.where(lane < 64, got[0], got[1])
            into[i, b] += jnp.where((at >= c) & (at < end), source, 0.0)

    def prepare(s, _):
        p, c, end = place(s)
        amp[s] = permuted_amp(frames[idx_ref[0, s]])
        lane = lanes(PS)
        turn = lax.rem(c + PS, PS)
        by = lax.rem(turn, 128)
        swap = lax.div(turn, 128)
        other = (1 - 2 * swap) * (lane - by) - swap < 0
        kept = []
        for i in range(2):
            a, b = (turns[lax.div(by, 16), i, h] for h in (0, 1))
            kept.append((jnp.where(other, b, a), jnp.where(other, a, b)))
            for h in range(2):
                wave[s, i, h] = kept[i][h]
        for h in range(2):
            power = kept[0][h] * kept[0][h] + kept[1][h] * kept[1][h]
            term[0, h, 12:28] = power.reshape(16, 16, 128)
        add(light, 0, p, c, end)
        return 0

    lax.fori_loop(0, SLOTS, prepare, 0)

    def pack_spill(ref, side_o, corner_o):
        for i in range(ref.shape[0]):
            for h in range(2):
                side_o[h, i] = pack(ref[i, 4, HALO : HALO + TR, :], h == 0)
            for k in range(4, 8):
                dr, dc = SIDES[k]
                at = 0 if dr < 0 else HALO + TR
                corner_o[k - 4, i] = pack(ref[i, 4, at : at + HALO, :], dc < 0)

    pack_spill(light, lside_out, lcorner_out)

    arrive(objects)
    for i in range(2):
        for at, rows, low, high in (
            (0, HALO, corner_in[1, i], corner_in[0, i]),
            (HALO, TR, side_in[1, i], side_in[0, i]),
            (HALO + TR, HALO, corner_in[3, i], corner_in[2, i]),
        ):
            edge = jnp.where(lanes(rows) < 64, unpack(low, False), unpack(high, True))
            po[i, 4, at // 16 : (at + rows) // 16] = edge.reshape(rows // 16, 16, 128)
    start(lights)

    def step(s, _):
        p, c, end = place(s)
        lane = lanes(PS)
        blocks = []
        for i in range(2):
            here = [po[i, b, pl.ds(p, 16)].reshape(PS, 128) for b in range(5)]
            first = jnp.where(lane >= c, here[0], jnp.where(lane + 256 >= c, here[2], here[4]))
            second = jnp.where(lane - 128 >= c, here[4], jnp.where(lane + 128 >= c, here[1], here[3]))
            blocks.append((first, second))
        wr, wi = ([wave[s, i, h] for h in range(2)] for i in range(2))
        t_re, t_im = slot_terms(blocks, wr, wi, amp[s], tab)
        for i, t in enumerate((t_re, t_im)):
            for h in range(2):
                term[i, h, 12:28] = t[h].reshape(16, 16, 128)
        for i in range(2):
            add(acc, i, p, c, end)
        return 0

    lax.fori_loop(0, SLOTS, step, 0)

    pack_spill(acc, gside_out, gcorner_out)
    start(grads)

    def absorb(ref, row_in, side_i, corner_i):
        for i in range(ref.shape[0]):
            for h, at in ((0, HALO), (1, TR)):
                ref[i, 0:4, at : at + HALO, :] += row_in[h, i]
            for h, b in ((0, 0), (1, 3)):
                keep = lanes(TR) < 32 if h == 0 else lanes(TR) >= 96
                ref[i, b, HALO : HALO + TR, :] += jnp.where(keep, unpack(side_i[h, i], h == 1), 0.0)
            for k in range(4, 8):
                dr, dc = SIDES[k]
                at = HALO if dr < 0 else TR
                keep = lanes(HALO) < 32 if dc < 0 else lanes(HALO) >= 96
                ref[i, 0 if dc < 0 else 3, at : at + HALO, :] += jnp.where(keep, unpack(corner_i[k - 4, i], dc > 0), 0.0)

    arrive(lights)
    absorb(light, lrow_in, lside_in, lcorner_in)
    for b in range(4):
        light[0, b, HALO : HALO + TR, :] = 1.0 / (light[0, b, HALO : HALO + TR, :] + 1.0)
    arrive(grads)
    absorb(acc, grow_in, gside_in, gcorner_in)
    for i, out in enumerate((new_re, new_im)):
        for b in range(4):
            rows = pl.ds(HALO, TR)
            out[:, 128 * b : 128 * b + 128] = po[i, b, 2:26].reshape(TR, 128) - acc[i, b, rows, :] * light[0, b, rows, :]
    for group in (objects, lights, grads):
        drain(group)


def shards(object_re, object_im, probe_re, probe_im, frames, counts, offsets, frame_index):
    smem = pl.BlockSpec(memory_space=pltpu.SMEM)
    anywhere = pl.BlockSpec(memory_space=pl.ANY)
    vmem = pl.BlockSpec(memory_space=pltpu.VMEM)
    spills = []
    for n in (1, 2):
        spills += [
            pltpu.VMEM((2, n, 4, HALO, 128), F32),
            pltpu.VMEM((2, n, 96, 128), F32),
            pltpu.VMEM((2, n, 96, 128), F32),
            pltpu.VMEM((4, n, 8, 128), F32),
            pltpu.VMEM((4, n, 8, 128), F32),
        ]
    return pl.pallas_call(
        kernel,
        out_shape=(jax.ShapeDtypeStruct((TR, TC), F32),) * 2,
        in_specs=[smem] * 3 + [anywhere] * 6,
        out_specs=(vmem, vmem),
        scratch_shapes=[
            pltpu.VMEM((2, 5, 28, 16, 128), F32),
            pltpu.VMEM((2, 5, WIDE, 128), F32),
            pltpu.VMEM((1, 5, WIDE, 128), F32),
            pltpu.VMEM((2, 2, 40, 16, 128), F32),
            pltpu.VMEM((SLOTS, PS, PS), F32),
            pltpu.VMEM((SLOTS, 2, 2, PS, 128), F32),
            pltpu.VMEM((8, 2, 2, PS, 128), F32),
            pltpu.VMEM((8, PS, PS), BF16),
            pltpu.VMEM((4, 2, PS, PS), BF16),
            pltpu.VMEM((2, PS, PS), F32),
            pltpu.VMEM((2, 2, 96, 128), F32),
            pltpu.VMEM((2, 2, 96, 128), F32),
            pltpu.VMEM((4, 2, 8, 128), F32),
            pltpu.VMEM((4, 2, 8, 128), F32),
            *spills,
            pltpu.SemaphoreType.DMA((12,)),
            pltpu.SemaphoreType.DMA((3, 8)),
            pltpu.SemaphoreType.DMA((3, 8)),
        ],
        compiler_params=pltpu.CompilerParams(
            collective_id=0, has_side_effects=True, vmem_limit_bytes=63 << 20
        ),
    )(
        counts, offsets[0, 0].T, frame_index.reshape(1, SLOTS),
        object_re.reshape(24, 16, TC), object_im.reshape(24, 16, TC), probe_re, probe_im, frames.reshape(8, PS, PS), jnp.asarray(tables()),
    )


def solution(mesh):
    return jax.shard_map(
        shards,
        mesh=mesh,
        in_specs=(
            P("row", "col"),
            P("row", "col"),
            P(),
            P(),
            P("row", "col", None, None, None),
            P("row", "col"),
            P("row", "col", None, None),
            P("row", "col", None),
        ),
        out_specs=(P("row", "col"), P("row", "col")),
        check_vma=False,
    )
```

profile of v0, /device:TPU:59, one launch (start us, length us, event | category | flops | bytes accessed | tf_op | source)
XLA Modules:
  0.0 49.4 jit_solution(3934271424060001120)
XLA Ops:
  1.3 45.0 %shard_map.104 = (f32[384,512]{1,0:T(8,128)}, f32[384,512]{1,0:T(8,128)}) custom-call(s32[1,1]{1,0:T(1,128)S(6)} %copy.13.count_ref, s32[2,8]{1,0:T(2,128)} %bitcast.10, s32[1,8]{1,0:T(1,128)} %bitcast.11, f32[24,16,512]{2,1,0:T(8,128)} %bitcast.8, f32[24,16,512]{2,1,0:T(8,128)} %bitcast.9, f32[256,256]{1,0:T(8,128)} %probe_re.1, f32[256,256]{1,0:T(8,128)} %probe_im.1, ...), custom_call_target="tpu_custom_call" | custom-call | tf_op jit(solution)/shard_map/pallas_call | solution.py:375
  46.3 0.0 copy-start
  46.3 2.1 %copy.14 = f32[384,512]{1,0:T(8,128)} copy(f32[384,512]{1,0:T(8,128)} %get-tuple-element.4) | data formatting | bytes 1572864
  48.5 0.0 copy-done
  48.5 0.9 %copy.15 = f32[384,512]{1,0:T(8,128)} copy(f32[384,512]{1,0:T(8,128)S(1)} %copy-done) | data formatting | bytes 1572864
Async XLA Ops:
  46.3 2.1 %copy-start = (f32[384,512]{1,0:T(8,128)S(1)}, f32[384,512]{1,0:T(8,128)}, u32[]{:S(2)}) copy-start(f32[384,512]{1,0:T(8,128)} %get-tuple-element.5) | copy-start | bytes 2359300
where the time goes:
time: 49.5 us; the launch traced here: 49.4 us
  Pallas kernels  45 us (91%)
  local copies, waits for them, and re-layouts  3.02 us (6%)
  between operations  1.29 us (3%)
    pallas_call x1, Pallas kernels, shards(): pl.pallas_call(kernel, out_shape=(jax.ShapeDtypeStruct((TR, TC), F32),) *...  45 us
    unnamed x4, local copies, waits for them, and re-layouts  3.02 us

commit v1 on v0

--- a/solution.py
+++ b/solution.py
@@ -8,6 +8,7 @@
 
 F32, BF16 = jnp.float32, jnp.bfloat16
 HALO, TR, TC, PS, SLOTS = 32, 384, 512, 256, 8
+ROWS = 32
 WIDE = TR + 2 * HALO
 SIDES = ((-1, 0), (1, 0), (0, -1), (0, 1), (-1, -1), (-1, 1), (1, -1), (1, 1))
 BACK = tuple(SIDES.index((-r, -c)) for r, c in SIDES)
@@ -38,22 +39,29 @@
 
 
 def right(x, tab, t):
-    hi, lo = split(x)
+    hi, lo = x
     th, tl = tab[t, 0], tab[t, 1]
     return dot(jnp.concatenate([hi, lo, hi], 1), jnp.concatenate([th, th, tl], 0))
 
 
 def left(x, tab, t):
-    hi, lo = split(x)
+    hi, lo = x
     th, tl = tab[t, 0], tab[t, 1]
     return dot(jnp.concatenate([th, th, tl], 1), jnp.concatenate([hi, lo, hi], 0))
 
 
-def slot_terms(blocks, wr, wi, amp, tab):
+def slot_terms(patch, wave, amp, tab, keep):
+    wr, wi = wave()
+    blocks = patch()
     e_re = [wr[b] * blocks[0][b] - wi[b] * blocks[1][b] for b in (0, 1)]
     e_im = [wr[b] * blocks[1][b] + wi[b] * blocks[0][b] for b in (0, 1)]
-    even = right(jnp.concatenate([e_re[0] + e_re[1], e_im[0] + e_im[1]], 1), tab, 0)
-    odd = right(jnp.concatenate([e_re[0] - e_re[1], e_im[0] - e_im[1]], 1), tab, 2)
+    even = jnp.concatenate([e_re[0] + e_re[1], e_im[0] + e_im[1]], 1)
+    odd = jnp.concatenate([e_re[0] - e_re[1], e_im[0] - e_im[1]], 1)
+    even, odd = split(even), split(odd)
+    yield
+    even = right(even, tab, 0)
+    odd = right(odd, tab, 2)
+    yield
 
     def halves(op):
         a, b = op(even[:128], even[128:]), op(odd[:128], odd[128:])
@@ -61,37 +69,48 @@
         im = jnp.concatenate([a[:, 128:], b[:, 128:]], 1)
         return jnp.concatenate([re, im], 0)
 
-    u = left(halves(lambda p, q: p + q), tab, 1)
-    v = left(halves(lambda p, q: p - q), tab, 3)
+    u, v = split(halves(lambda p, q: p + q)), split(halves(lambda p, q: p - q))
+    yield
+    u = left(u, tab, 1)
+    v = left(v, tab, 3)
+    yield
 
     def scaled(f, a):
         re, im = f[:128], f[128:]
         factor = 1.0 - a * lax.rsqrt(jnp.maximum(re * re + im * im, 0.25))
-        return jnp.concatenate([re * factor, im * factor], 0)
-
-    a = left(scaled(u, amp[:128]), tab, 0)
-    b = left(scaled(v, amp[128:]), tab, 2)
+        return split(jnp.concatenate([re * factor, im * factor], 0))
+
+    a, b = amp()
+    u, v = scaled(u, a), scaled(v, b)
+    yield
+    a = left(u, tab, 0)
+    b = left(v, tab, 2)
+    yield
     top, bot = a + b, a - b
     re = jnp.concatenate([top[:128], bot[:128]], 0)
     im = jnp.concatenate([top[128:], bot[128:]], 0)
-    a = right(jnp.concatenate([re[:, :128], im[:, :128]], 1), tab, 1)
-    b = right(jnp.concatenate([re[:, 128:], im[:, 128:]], 1), tab, 3)
+    u = split(jnp.concatenate([re[:, :128], im[:, :128]], 1))
+    v = split(jnp.concatenate([re[:, 128:], im[:, 128:]], 1))
+    yield
+    a = right(u, tab, 1)
+    b = right(v, tab, 3)
+    yield
     back = (a + b, a - b)
-    t_re = [wr[i] * back[i][:, :128] + wi[i] * back[i][:, 128:] for i in (0, 1)]
-    t_im = [wr[i] * back[i][:, 128:] - wi[i] * back[i][:, :128] for i in (0, 1)]
-    return t_re, t_im
-
-
-def permuted_amp(frame):
+    wr, wi = wave()
+    for i in (0, 1):
+        keep(0, i, wr[i] * back[i][:, :128] + wi[i] * back[i][:, 128:])
+        keep(1, i, wr[i] * back[i][:, 128:] - wi[i] * back[i][:, :128])
+    yield
+
+
+def orders():
     r = lax.broadcasted_iota(jnp.int32, (PS, PS), 0)
     c = lax.broadcasted_iota(jnp.int32, (PS, PS), 1)
 
     def order(j):
         return jnp.where(j < 128, 2 * j, 2 * j - 255)
 
-    cols = (r == order(c)).astype(F32).astype(BF16)
-    rows = (c == order(r)).astype(F32).astype(BF16)
-    return jnp.sqrt(dot(rows, dot(frame, cols).astype(BF16)))
+    return (r == order(c)).astype(F32).astype(BF16), (c == order(r)).astype(F32).astype(BF16)
 
 
 def lanes(rows):
@@ -119,7 +138,7 @@
 def kernel(
     count_ref, off_ref, idx_ref, obj_re, obj_im, probe_re, probe_im, frames_hbm, tab_hbm,
     new_re, new_im,
-    po, acc, light, term, amp, wave, turns, frames, tab, probe,
+    po, acc, light, term, amp, wave, turns, frames, tab, probe, swaps, base,
     side_out, side_in, corner_out, corner_in,
     lrow_in, lside_out, lside_in, lcorner_out, lcorner_in,
     grow_in, gside_out, gside_in, gcorner_out, gcorner_in,
@@ -146,32 +165,11 @@
     loads = []
     for b in range(4):
         for i, source in enumerate((obj_re, obj_im)):
-            loads.append((source.at[:, :, pl.ds(128 * b, 128)], po.at[i, b, 2:26]))
+            loads.append((source.at[:, :, pl.ds(128 * b, 128)], po.at[i, b + 1, 2:26]))
     loads += [(probe_re, probe.at[0]), (probe_im, probe.at[1]), (frames_hbm, frames), (tab_hbm, tab)]
     loads = [pltpu.make_async_copy(s, d, local_sem.at[i]) for i, (s, d) in enumerate(loads)]
     for load in loads:
         load.start()
-
-    for k, (dr, dc) in enumerate(SIDES):
-        @pl.when(jnp.logical_not(there[k]))
-        def _():
-            if dc == 0:
-                at = 0 if dr < 0 else HALO + TR
-                po[:, 0:4, at // 16 : at // 16 + 2] = jnp.zeros((2, 4, 2, 16, 128), F32)
-                h = 0 if dr < 0 else 1
-                lrow_in[h] = jnp.zeros((1, 4, HALO, 128), F32)
-                grow_in[h] = jnp.zeros((2, 4, HALO, 128), F32)
-            elif dr == 0:
-                for ref in (side_in, lside_in, gside_in):
-                    ref[k - 2] = jnp.zeros(ref.shape[1:], F32)
-            else:
-                for ref in (corner_in, lcorner_in, gcorner_in):
-                    ref[k - 4] = jnp.zeros(ref.shape[1:], F32)
-
-    acc[...] = jnp.zeros_like(acc)
-    light[...] = jnp.zeros_like(light)
-    term[:, :, 0:12] = jnp.zeros((2, 2, 12, 16, 128), F32)
-    term[:, :, 28:40] = jnp.zeros((2, 2, 12, 16, 128), F32)
 
     def message(phase, k, source, target):
         return pltpu.make_async_remote_copy(
@@ -215,8 +213,8 @@
 
     def object_rows(k):
         if k == 0:
-            return po.at[:, 0:4, 2:4], po.at[:, 0:4, 26:28]
-        return po.at[:, 0:4, 24:26], po.at[:, 0:4, 0:2]
+            return po.at[:, 1:5, 2:4], po.at[:, 1:5, 26:28]
+        return po.at[:, 1:5, 24:26], po.at[:, 1:5, 0:2]
 
     def spilled_rows(ref, into):
         def rows_of(k):
@@ -231,61 +229,128 @@
     for load in loads[:8]:
         load.wait()
     for i in range(2):
-        side_out[0, i] = pack(po[i, 0, 2:26].reshape(TR, 128), False)
-        side_out[1, i] = pack(po[i, 3, 2:26].reshape(TR, 128), True)
+        side_out[0, i] = pack(po[i, 1, 2:26].reshape(TR, 128), False)
+        side_out[1, i] = pack(po[i, 4, 2:26].reshape(TR, 128), True)
         for k in range(4, 8):
             dr, dc = SIDES[k]
             at = 2 if dr < 0 else 24
-            corner_out[k - 4, i] = pack(po[i, 0 if dc < 0 else 3, at : at + 2].reshape(HALO, 128), dc > 0)
+            corner_out[k - 4, i] = pack(po[i, 1 if dc < 0 else 4, at : at + 2].reshape(HALO, 128), dc > 0)
 
     neighbours = sum(t.astype(jnp.int32) for t in there)
     pl.semaphore_wait(barrier, neighbours)
     start(objects)
+
+    for k, (dr, dc) in enumerate(SIDES):
+        @pl.when(jnp.logical_not(there[k]))
+        def _():
+            if dc == 0:
+                at = 0 if dr < 0 else 26
+                po[:, 1:5, at : at + 2] = jnp.zeros((2, 4, 2, 16, 128), F32)
+                h = 0 if dr < 0 else 1
+                lrow_in[h] = jnp.zeros((1, 4, HALO, 128), F32)
+                grow_in[h] = jnp.zeros((2, 4, HALO, 128), F32)
+            elif dr == 0:
+                for ref in (side_in, lside_in, gside_in):
+                    ref[k - 2] = jnp.zeros(ref.shape[1:], F32)
+            else:
+                for ref in (corner_in, lcorner_in, gcorner_in):
+                    ref[k - 4] = jnp.zeros(ref.shape[1:], F32)
+
+    def clear(j, _):
+        for i in range(2):
+            term[i, pl.ds(40 * j, 12)] = jnp.zeros((12, 16, 128), F32)
+            term[i, pl.ds(40 * j + 28, 12)] = jnp.zeros((12, 16, 128), F32)
+        return 0
+
+    lax.fori_loop(0, 3 * SLOTS + 1, clear, 0)
+    for i in range(2):
+        term[i, 120 * SLOTS + 12 : 120 * SLOTS + 28] = jnp.zeros((16, 16, 128), F32)
+    swaps[0], swaps[1] = orders()
+
     for load in loads[8:]:
         load.wait()
-
     for i in range(2):
         for h in range(2):
             for k in range(8):
                 turns[k, i, h] = turned(probe[i, :, 128 * h : 128 * h + 128], 16 * k)
     count = count_ref[0, 0]
 
+    def unit(x):
+        return lax.max(lax.min(x, 1), 0)
+
     def place(s):
         p = lax.div(off_ref[0, s] + HALO, 16)
-        c = off_ref[1, s]
-        live = lax.max(lax.min(count - s, 1), 0)
-        return p, c, c + PS * live
-
-    def add(into, i, p, c, end):
-        rows = pl.ds(12 - p, 28)
-        lane = lanes(WIDE)
-        cols = [lane + 128 * b for b in range(4)] + [jnp.where(lane < 64, lane + 512, lane - 128)]
-        got = [term[i, h, rows].reshape(WIDE, 128) for h in range(2)]
-        for b, at in enumerate(cols):
-            source = got[b % 2] if b < 4 else jnp.where(lane < 64, got[0], got[1])
-            into[i, b] += jnp.where((at >= c) & (at < end), source, 0.0)
+        c = off_ref[1, s] + 128
+        return p, lax.div(c, 128), lax.rem(c, 128)
+
+    for s in range(SLOTS):
+        p, q, _ = place(s)
+        for b in range(6):
+            j = b - q
+            inside = unit(j + 1) * unit(3 - j) * unit(count - s)
+            block = 3 * SLOTS + inside * (3 * s + j - 3 * SLOTS)
+            base[6 * s + b] = 40 * block + 12 - p
+
+    def total(i, b, at, groups):
+        out = None
+        for s in range(SLOTS):
+            piece = term[i, pl.ds(base[6 * s + b] + at, groups)]
+            out = piece if out is None else out + piece
+        return out.reshape(16 * groups, 128)
+
+    def spill(into, i):
+        for b in range(4):
+            for at in (0, 26):
+                into[i, b, 16 * at : 16 * at + 32, :] = total(i, b + 1, at, 2)
+
+        def edge(g, _):
+            both = jnp.where(lanes(64) < 64, total(i, 5, 4 * g, 4), total(i, 0, 4 * g, 4))
+            into[i, 4, pl.ds(pl.multiple_of(64 * g, 64), 64), :] = both
+            return 0
+
+        lax.fori_loop(0, 7, edge, 0)
+
+    def inner(into, i):
+        def rows(g, _):
+            for b in range(4):
+                into[i, b, pl.ds(pl.multiple_of(HALO + 64 * g, 32), 64), :] = total(i, b + 1, 2 + 4 * g, 4)
+            return 0
+
+        lax.fori_loop(0, 6, rows, 0)
+
+    def keep(s, i, r, at, h, value):
+        def at_block(j):
+            return pl.ds(120 * s + (40 * j + 12 + at // 16), value.shape[0] // 16)
+
+        shape = (value.shape[0] // 16, 16, 128)
+        if h == 1:
+            term[i, at_block(1)] = value.reshape(shape)
+            return
+        mine = lanes(value.shape[0]) >= r
+        term[i, at_block(0)] = jnp.where(mine, value, 0.0).reshape(shape)
+        term[i, at_block(2)] = jnp.where(mine, 0.0, value).reshape(shape)
 
     def prepare(s, _):
-        p, c, end = place(s)
-        amp[s] = permuted_amp(frames[idx_ref[0, s]])
-        lane = lanes(PS)
-        turn = lax.rem(c + PS, PS)
-        by = lax.rem(turn, 128)
-        swap = lax.div(turn, 128)
-        other = (1 - 2 * swap) * (lane - by) - swap < 0
-        kept = []
-        for i in range(2):
-            a, b = (turns[lax.div(by, 16), i, h] for h in (0, 1))
-            kept.append((jnp.where(other, b, a), jnp.where(other, a, b)))
+        _, _, r = place(s)
+        mixed = dot(frames[idx_ref[0, s]], swaps[0]).astype(BF16)
+        amp[s] = jnp.sqrt(dot(swaps[1], mixed))
+        by = lax.div(r, 16)
+        for at in range(0, PS, ROWS):
+            rows = slice(at, at + ROWS)
+            other = lanes(ROWS) < r
+            kept = []
+            for i in range(2):
+                a, b = (turns[by, i, h, rows, :] for h in (0, 1))
+                kept.append((jnp.where(other, b, a), jnp.where(other, a, b)))
+                for h in range(2):
+                    wave[s, i, h, rows, :] = kept[i][h]
             for h in range(2):
-                wave[s, i, h] = kept[i][h]
-        for h in range(2):
-            power = kept[0][h] * kept[0][h] + kept[1][h] * kept[1][h]
-            term[0, h, 12:28] = power.reshape(16, 16, 128)
-        add(light, 0, p, c, end)
+                keep(s, 0, r, at, h, kept[0][h] * kept[0][h] + kept[1][h] * kept[1][h])
         return 0
 
     lax.fori_loop(0, SLOTS, prepare, 0)
+    spill(light, 0)
+    inner(light, 0)
 
     def pack_spill(ref, side_o, corner_o):
         for i in range(ref.shape[0]):
@@ -305,32 +370,44 @@
             (HALO, TR, side_in[1, i], side_in[0, i]),
             (HALO + TR, HALO, corner_in[3, i], corner_in[2, i]),
         ):
-            edge = jnp.where(lanes(rows) < 64, unpack(low, False), unpack(high, True))
-            po[i, 4, at // 16 : (at + rows) // 16] = edge.reshape(rows // 16, 16, 128)
+            for b, side in ((5, unpack(low, False)), (0, unpack(high, True))):
+                po[i, b, at // 16 : (at + rows) // 16] = side.reshape(rows // 16, 16, 128)
     start(lights)
 
-    def step(s, _):
-        p, c, end = place(s)
-        lane = lanes(PS)
-        blocks = []
-        for i in range(2):
-            here = [po[i, b, pl.ds(p, 16)].reshape(PS, 128) for b in range(5)]
-            first = jnp.where(lane >= c, here[0], jnp.where(lane + 256 >= c, here[2], here[4]))
-            second = jnp.where(lane - 128 >= c, here[4], jnp.where(lane + 128 >= c, here[1], here[3]))
-            blocks.append((first, second))
-        wr, wi = ([wave[s, i, h] for h in range(2)] for i in range(2))
-        t_re, t_im = slot_terms(blocks, wr, wi, amp[s], tab)
-        for i, t in enumerate((t_re, t_im)):
-            for h in range(2):
-                term[i, h, 12:28] = t[h].reshape(16, 16, 128)
-        for i in range(2):
-            add(acc, i, p, c, end)
+    def slot(s):
+        p, q, r = place(s)
+
+        def patch():
+            out = []
+            for i in range(2):
+                first, middle, last = (po[i, q + j, pl.ds(p, 16)].reshape(PS, 128) for j in range(3))
+                out.append((jnp.where(lanes(PS) >= r, first, last), middle))
+            return out
+
+        return slot_terms(
+            patch,
+            lambda: [[wave[s, i, h] for h in range(2)] for i in range(2)],
+            lambda: (amp[s, 0:128], amp[s, 128:256]),
+            tab,
+            lambda i, h, value: keep(s, i, r, 0, h, value),
+        )
+
+    def step(j, _):
+        first, second = slot(2 * j), slot(2 * j + 1)
+        next(first)
+        for _ in range(8):
+            next(second)
+            next(first)
+        next(second)
         return 0
 
-    lax.fori_loop(0, SLOTS, step, 0)
-
+    lax.fori_loop(0, SLOTS // 2, step, 0)
+    for i in range(2):
+        spill(acc, i)
     pack_spill(acc, gside_out, gcorner_out)
     start(grads)
+    for i in range(2):
+        inner(acc, i)
 
     def absorb(ref, row_in, side_i, corner_i):
         for i in range(ref.shape[0]):
@@ -354,9 +431,25 @@
     for i, out in enumerate((new_re, new_im)):
         for b in range(4):
             rows = pl.ds(HALO, TR)
-            out[:, 128 * b : 128 * b + 128] = po[i, b, 2:26].reshape(TR, 128) - acc[i, b, rows, :] * light[0, b, rows, :]
+            out[:, 128 * b : 128 * b + 128] = po[i, b + 1, 2:26].reshape(TR, 128) - acc[i, b, rows, :] * light[0, b, rows, :]
     for group in (objects, lights, grads):
         drain(group)
+
+
+def write_out(re, im, new_re, new_im, held, sem):
+    into, out = [], []
+    for i, (source, target) in enumerate(((re, new_re), (im, new_im))):
+        for j in range(4):
+            rows = pl.ds(96 * j, 96)
+            into.append(pltpu.make_async_copy(source.at[rows], held.at[i, rows], sem.at[0, i, j]))
+            out.append(pltpu.make_async_copy(held.at[i, rows], target.at[rows], sem.at[1, i, j]))
+    for copy in into:
+        copy.start()
+    for before, after in zip(into, out):
+        before.wait()
+        after.start()
+    for copy in out:
+        copy.wait()
 
 
 def shards(object_re, object_im, probe_re, probe_im, frames, counts, offsets, frame_index):
@@ -372,22 +465,24 @@
             pltpu.VMEM((4, n, 8, 128), F32),
             pltpu.VMEM((4, n, 8, 128), F32),
         ]
-    return pl.pallas_call(
+    results = pl.pallas_call(
         kernel,
         out_shape=(jax.ShapeDtypeStruct((TR, TC), F32),) * 2,
         in_specs=[smem] * 3 + [anywhere] * 6,
         out_specs=(vmem, vmem),
         scratch_shapes=[
-            pltpu.VMEM((2, 5, 28, 16, 128), F32),
+            pltpu.VMEM((2, 6, 28, 16, 128), F32),
             pltpu.VMEM((2, 5, WIDE, 128), F32),
             pltpu.VMEM((1, 5, WIDE, 128), F32),
-            pltpu.VMEM((2, 2, 40, 16, 128), F32),
+            pltpu.VMEM((2, 40 * (3 * SLOTS + 1), 16, 128), F32),
             pltpu.VMEM((SLOTS, PS, PS), F32),
             pltpu.VMEM((SLOTS, 2, 2, PS, 128), F32),
             pltpu.VMEM((8, 2, 2, PS, 128), F32),
             pltpu.VMEM((8, PS, PS), BF16),
             pltpu.VMEM((4, 2, PS, PS), BF16),
             pltpu.VMEM((2, PS, PS), F32),
+            pltpu.VMEM((2, PS, PS), BF16),
+            pltpu.SMEM((6 * SLOTS,), jnp.int32),
             pltpu.VMEM((2, 2, 96, 128), F32),
             pltpu.VMEM((2, 2, 96, 128), F32),
             pltpu.VMEM((4, 2, 8, 128), F32),
@@ -404,6 +499,14 @@
         counts, offsets[0, 0].T, frame_index.reshape(1, SLOTS),
         object_re.reshape(24, 16, TC), object_im.reshape(24, 16, TC), probe_re, probe_im, frames.reshape(8, PS, PS), jnp.asarray(tables()),
     )
+    return pl.pallas_call(
+        write_out,
+        out_shape=(jax.ShapeDtypeStruct((TR, TC), F32),) * 2,
+        in_specs=[anywhere] * 2,
+        out_specs=(anywhere,) * 2,
+        scratch_shapes=[pltpu.VMEM((2, TR, TC), F32), pltpu.SemaphoreType.DMA((2, 2, 4))],
+        compiler_params=pltpu.CompilerParams(vmem_limit_bytes=63 << 20),
+    )(*results)
 
 
 def solution(mesh):

time: 49.5 us -> 42.5 us (0.86)
  the two profiles are of different devices: /device:TPU:59 before, /device:TPU:61 now
where the time goes in v1:
time: 42.5 us; the launch traced here: 42.4 us
  Pallas kernels  41.1 us (97%)
  between operations  1.29 us (3%)
    pallas_call x1, Pallas kernels, shards(): pl.pallas_call(kernel, out_shape=(jax.ShapeDtypeStruct((TR, TC), F32),) *...  38.8 us
    pallas_call x1, Pallas kernels, shards(): pl.pallas_call(write_out, out_shape=(jax.ShapeDtypeStruct((TR, TC), F32),...  2.29 us

profile of v1, /device:TPU:61, one launch (start us, length us, event | category | flops | bytes accessed | tf_op | source)
XLA Modules:
  0.0 42.4 jit_solution(5231022636149506337)
XLA Ops:
  1.3 38.8 %shard_map.104 = (f32[384,512]{1,0:T(8,128)}, f32[384,512]{1,0:T(8,128)}) custom-call(s32[1,1]{1,0:T(1,128)S(6)} %copy.11.count_ref, s32[2,8]{1,0:T(2,128)} %bitcast.10, s32[1,8]{1,0:T(1,128)} %bitcast.11, f32[24,16,512]{2,1,0:T(8,128)} %bitcast.8, f32[24,16,512]{2,1,0:T(8,128)} %bitcast.9, f32[256,256]{1,0:T(8,128)} %probe_re.1, f32[256,256]{1,0:T(8,128)} %probe_im.1, ...), custom_call_target="tpu_custom_call" | custom-call | tf_op jit(solution)/shard_map/pallas_call | solution.py:468
  40.1 2.3 %shard_map.105 = (f32[384,512]{1,0:T(8,128)}, f32[384,512]{1,0:T(8,128)}) custom-call(f32[384,512]{1,0:T(8,128)} %get-tuple-element.4.re, f32[384,512]{1,0:T(8,128)} %get-tuple-element.5.im), custom_call_target="tpu_custom_call" | custom-call | tf_op jit(solution)/shard_map/pallas_call | solution.py:502

commit v2 on v1

--- a/solution.py
+++ b/solution.py
@@ -136,13 +136,13 @@
 
 
 def kernel(
-    count_ref, off_ref, idx_ref, obj_re, obj_im, probe_re, probe_im, frames_hbm, tab_hbm,
+    count_hbm, off_hbm, idx_hbm, obj_re, obj_im, probe_re, probe_im, frames_hbm, tab_hbm,
     new_re, new_im,
     po, acc, light, term, amp, wave, turns, frames, tab, probe, swaps, base,
     side_out, side_in, corner_out, corner_in,
     lrow_in, lside_out, lside_in, lcorner_out, lcorner_in,
     grow_in, gside_out, gside_in, gcorner_out, gcorner_in,
-    local_sem, send_sem, recv_sem,
+    count_ref, off_ref, idx_ref, newv, local_sem, send_sem, recv_sem, out_sem,
 ):
     row, col = lax.axis_index("row"), lax.axis_index("col")
     n_row, n_col = lax.axis_size("row"), lax.axis_size("col")
@@ -163,10 +163,11 @@
             pl.semaphore_signal(barrier, inc=1, device_id=peers[k], device_id_type=pl.DeviceIdType.MESH)
 
     loads = []
-    for b in range(4):
+    for b in (0, 3, 1, 2):
         for i, source in enumerate((obj_re, obj_im)):
             loads.append((source.at[:, :, pl.ds(128 * b, 128)], po.at[i, b + 1, 2:26]))
     loads += [(probe_re, probe.at[0]), (probe_im, probe.at[1]), (frames_hbm, frames), (tab_hbm, tab)]
+    loads += [(count_hbm, count_ref), (off_hbm, off_ref), (idx_hbm, idx_ref)]
     loads = [pltpu.make_async_copy(s, d, local_sem.at[i]) for i, (s, d) in enumerate(loads)]
     for load in loads:
         load.start()
@@ -193,8 +194,8 @@
                 out.append(message(phase, k, corner_o.at[k - 4], corner_i.at[j - 4]))
         return out
 
-    def start(group):
-        for k in range(8):
+    def start(group, some=range(8)):
+        for k in some:
             @pl.when(there[k])
             def _():
                 group[k].start()
@@ -226,7 +227,7 @@
     lights = messages(1, spilled_rows(light, lrow_in), lside_out, lside_in, lcorner_out, lcorner_in)
     grads = messages(2, spilled_rows(acc, grow_in), gside_out, gside_in, gcorner_out, gcorner_in)
 
-    for load in loads[:8]:
+    for load in loads[:4]:
         load.wait()
     for i in range(2):
         side_out[0, i] = pack(po[i, 1, 2:26].reshape(TR, 128), False)
@@ -236,6 +237,8 @@
             at = 2 if dr < 0 else 24
             corner_out[k - 4, i] = pack(po[i, 1 if dc < 0 else 4, at : at + 2].reshape(HALO, 128), dc > 0)
 
+    for load in loads[4:8]:
+        load.wait()
     neighbours = sum(t.astype(jnp.int32) for t in there)
     pl.semaphore_wait(barrier, neighbours)
     start(objects)
@@ -298,11 +301,12 @@
             out = piece if out is None else out + piece
         return out.reshape(16 * groups, 128)
 
-    def spill(into, i):
+    def spill_rows(into, i):
         for b in range(4):
             for at in (0, 26):
                 into[i, b, 16 * at : 16 * at + 32, :] = total(i, b + 1, at, 2)
 
+    def spill_edge(into, i):
         def edge(g, _):
             both = jnp.where(lanes(64) < 64, total(i, 5, 4 * g, 4), total(i, 0, 4 * g, 4))
             into[i, 4, pl.ds(pl.multiple_of(64 * g, 64), 64), :] = both
@@ -349,7 +353,8 @@
         return 0
 
     lax.fori_loop(0, SLOTS, prepare, 0)
-    spill(light, 0)
+    spill_rows(light, 0)
+    spill_edge(light, 0)
     inner(light, 0)
 
     def pack_spill(ref, side_o, corner_o):
@@ -403,9 +408,12 @@
 
     lax.fori_loop(0, SLOTS // 2, step, 0)
     for i in range(2):
-        spill(acc, i)
+        spill_rows(acc, i)
+    start(grads, (0, 1))
+    for i in range(2):
+        spill_edge(acc, i)
     pack_spill(acc, gside_out, gcorner_out)
-    start(grads)
+    start(grads, range(2, 8))
     for i in range(2):
         inner(acc, i)
 
@@ -426,12 +434,40 @@
     absorb(light, lrow_in, lside_in, lcorner_in)
     for b in range(4):
         light[0, b, HALO : HALO + TR, :] = 1.0 / (light[0, b, HALO : HALO + TR, :] + 1.0)
+    rows = pl.ds(HALO, TR)
+    outs = (new_re, new_im)
+    for i in range(2):
+        for b in range(4):
+            mine = po[i, b + 1, 2:26].reshape(TR, 128) - acc[i, b, rows, :] * light[0, b, rows, :]
+            newv[i, :, 128 * b : 128 * b + 128] = mine
+
+    def leave(i, j, down, across):
+        return pltpu.make_async_copy(newv.at[i, down, across], outs[i].at[down, across], out_sem.at[i, j])
+
+    middle = pl.ds(HALO, TR - 2 * HALO)
+    first = [leave(i, 0, middle, pl.ds(128, 256)) for i in range(2)]
+    last = []
+    for i in range(2):
+        last += [leave(i, 1, pl.ds(0, HALO), pl.ds(0, TC)), leave(i, 2, pl.ds(TR - HALO, HALO), pl.ds(0, TC))]
+        last += [leave(i, 3, middle, pl.ds(0, 128)), leave(i, 4, middle, pl.ds(384, 128))]
+    for copy in first:
+        copy.start()
     arrive(grads)
-    absorb(acc, grow_in, gside_in, gcorner_in)
-    for i, out in enumerate((new_re, new_im)):
-        for b in range(4):
-            rows = pl.ds(HALO, TR)
-            out[:, 128 * b : 128 * b + 128] = po[i, b + 1, 2:26].reshape(TR, 128) - acc[i, b, rows, :] * light[0, b, rows, :]
+    for i in range(2):
+        for h, at in ((0, 0), (1, TR - HALO)):
+            for b in range(4):
+                newv[i, at : at + HALO, 128 * b : 128 * b + 128] -= grow_in[h, i, b] * light[0, b, HALO + at : 2 * HALO + at, :]
+        for h, b in ((0, 0), (1, 3)):
+            across = slice(128 * b, 128 * b + 128)
+            part = unpack(gside_in[h, i], h == 1)
+            ends = [unpack(gcorner_in[2 * v + h, i], h == 1) for v in range(2)]
+            low = jnp.concatenate([part[:HALO] + ends[0], part[HALO : TR - HALO], part[TR - HALO :] + ends[1]], 0)
+            keep_lanes = lanes(TR) < 32 if h == 0 else lanes(TR) >= 96
+            newv[i, :, across] -= jnp.where(keep_lanes, low * light[0, b, rows, :], 0.0)
+    for copy in last:
+        copy.start()
+    for copy in first + last:
+        copy.wait()
     for group in (objects, lights, grads):
         drain(group)
 
@@ -439,8 +475,8 @@
 def write_out(re, im, new_re, new_im, held, sem):
     into, out = [], []
     for i, (source, target) in enumerate(((re, new_re), (im, new_im))):
-        for j in range(4):
-            rows = pl.ds(96 * j, 96)
+        for j in range(8):
+            rows = pl.ds(48 * j, 48)
             into.append(pltpu.make_async_copy(source.at[rows], held.at[i, rows], sem.at[0, i, j]))
             out.append(pltpu.make_async_copy(held.at[i, rows], target.at[rows], sem.at[1, i, j]))
     for copy in into:
@@ -453,9 +489,7 @@
 
 
 def shards(object_re, object_im, probe_re, probe_im, frames, counts, offsets, frame_index):
-    smem = pl.BlockSpec(memory_space=pltpu.SMEM)
     anywhere = pl.BlockSpec(memory_space=pl.ANY)
-    vmem = pl.BlockSpec(memory_space=pltpu.VMEM)
     spills = []
     for n in (1, 2):
         spills += [
@@ -468,8 +502,8 @@
     results = pl.pallas_call(
         kernel,
         out_shape=(jax.ShapeDtypeStruct((TR, TC), F32),) * 2,
-        in_specs=[smem] * 3 + [anywhere] * 6,
-        out_specs=(vmem, vmem),
+        in_specs=[anywhere] * 9,
+        out_specs=(anywhere, anywhere),
         scratch_shapes=[
             pltpu.VMEM((2, 6, 28, 16, 128), F32),
             pltpu.VMEM((2, 5, WIDE, 128), F32),
@@ -488,9 +522,14 @@
             pltpu.VMEM((4, 2, 8, 128), F32),
             pltpu.VMEM((4, 2, 8, 128), F32),
             *spills,
-            pltpu.SemaphoreType.DMA((12,)),
+            pltpu.SMEM((1, 1), jnp.int32),
+            pltpu.SMEM((2, SLOTS), jnp.int32),
+            pltpu.SMEM((1, SLOTS), jnp.int32),
+            pltpu.VMEM((2, TR, TC), F32),
+            pltpu.SemaphoreType.DMA((15,)),
             pltpu.SemaphoreType.DMA((3, 8)),
             pltpu.SemaphoreType.DMA((3, 8)),
+            pltpu.SemaphoreType.DMA((2, 5)),
         ],
         compiler_params=pltpu.CompilerParams(
             collective_id=0, has_side_effects=True, vmem_limit_bytes=63 << 20
@@ -504,7 +543,7 @@
         out_shape=(jax.ShapeDtypeStruct((TR, TC), F32),) * 2,
         in_specs=[anywhere] * 2,
         out_specs=(anywhere,) * 2,
-        scratch_shapes=[pltpu.VMEM((2, TR, TC), F32), pltpu.SemaphoreType.DMA((2, 2, 4))],
+        scratch_shapes=[pltpu.VMEM((2, TR, TC), F32), pltpu.SemaphoreType.DMA((2, 2, 8))],
         compiler_params=pltpu.CompilerParams(vmem_limit_bytes=63 << 20),
     )(*results)
 

time: 42.5 us -> 41.3 us (0.972)
  the two profiles are of different devices: /device:TPU:61 before, /device:TPU:63 now
where the time goes in v2:
time: 41.3 us; the launch traced here: 41.1 us
  Pallas kernels  39.9 us (97%)
  between operations  1.29 us (3%)
    pallas_call x1, Pallas kernels, shards(): pl.pallas_call(kernel, out_shape=(jax.ShapeDtypeStruct((TR, TC), F32),) *...  37.5 us
    pallas_call x1, Pallas kernels, shards(): pl.pallas_call(write_out, out_shape=(jax.ShapeDtypeStruct((TR, TC), F32),...  2.4 us

profile of v2, /device:TPU:63, one launch (start us, length us, event | category | flops | bytes accessed | tf_op | source)
XLA Modules:
  0.0 41.1 jit_solution(17498485938833662173)
XLA Ops:
  1.3 37.5 %shard_map.104 = (f32[384,512]{1,0:T(8,128)}, f32[384,512]{1,0:T(8,128)}) custom-call(s32[1,1]{1,0:T(1,128)S(6)} %copy.11.count_hbm, s32[2,8]{1,0:T(2,128)} %bitcast.10, s32[1,8]{1,0:T(1,128)} %bitcast.11, f32[24,16,512]{2,1,0:T(8,128)} %bitcast.8, f32[24,16,512]{2,1,0:T(8,128)} %bitcast.9, f32[256,256]{1,0:T(8,128)} %probe_re.1, f32[256,256]{1,0:T(8,128)} %probe_im.1, ...), custom_call_target="tpu_custom_call" | custom-call | tf_op jit(solution)/shard_map/pallas_call | solution.py:502
  38.7 2.4 %shard_map.105 = (f32[384,512]{1,0:T(8,128)}, f32[384,512]{1,0:T(8,128)}) custom-call(f32[384,512]{1,0:T(8,128)} %get-tuple-element.4.re, f32[384,512]{1,0:T(8,128)} %get-tuple-element.5.im), custom_call_target="tpu_custom_call" | custom-call | tf_op jit(solution)/shard_map/pallas_call | solution.py:541

commit v3 on v2

--- a/solution.py
+++ b/solution.py
@@ -194,7 +194,7 @@
                 out.append(message(phase, k, corner_o.at[k - 4], corner_i.at[j - 4]))
         return out
 
-    def start(group, some=range(8)):
+    def start(group, some=(4, 5, 6, 7, 0, 1, 2, 3)):
         for k in some:
             @pl.when(there[k])
             def _():
@@ -413,7 +413,7 @@
     for i in range(2):
         spill_edge(acc, i)
     pack_spill(acc, gside_out, gcorner_out)
-    start(grads, range(2, 8))
+    start(grads, (4, 5, 6, 7, 2, 3))
     for i in range(2):
         inner(acc, i)
 

time: 41.3 us -> 40.6 us (0.983)
  the two profiles are of different devices: /device:TPU:63 before, /device:TPU:59 now
where the time goes in v3:
time: 40.6 us; the launch traced here: 40.4 us
  Pallas kernels  39.1 us (96%)
  between operations  1.29 us (3%)
    pallas_call x1, Pallas kernels, shards(): pl.pallas_call(kernel, out_shape=(jax.ShapeDtypeStruct((TR, TC), F32),) *...  36.7 us
    pallas_call x1, Pallas kernels, shards(): pl.pallas_call(write_out, out_shape=(jax.ShapeDtypeStruct((TR, TC), F32),...  2.4 us

profile of v3, /device:TPU:59, one launch (start us, length us, event | category | flops | bytes accessed | tf_op | source)
XLA Modules:
  0.0 40.4 jit_solution(13923827152664870574)
XLA Ops:
  1.3 36.7 %shard_map.104 = (f32[384,512]{1,0:T(8,128)}, f32[384,512]{1,0:T(8,128)}) custom-call(s32[1,1]{1,0:T(1,128)S(6)} %copy.11.count_hbm, s32[2,8]{1,0:T(2,128)} %bitcast.10, s32[1,8]{1,0:T(1,128)} %bitcast.11, f32[24,16,512]{2,1,0:T(8,128)} %bitcast.8, f32[24,16,512]{2,1,0:T(8,128)} %bitcast.9, f32[256,256]{1,0:T(8,128)} %probe_re.1, f32[256,256]{1,0:T(8,128)} %probe_im.1, ...), custom_call_target="tpu_custom_call" | custom-call | tf_op jit(solution)/shard_map/pallas_call | solution.py:502
  38.0 2.4 %shard_map.105 = (f32[384,512]{1,0:T(8,128)}, f32[384,512]{1,0:T(8,128)}) custom-call(f32[384,512]{1,0:T(8,128)} %get-tuple-element.4.re, f32[384,512]{1,0:T(8,128)} %get-tuple-element.5.im), custom_call_target="tpu_custom_call" | custom-call | tf_op jit(solution)/shard_map/pallas_call | solution.py:541
